TPU v7x, 512 devices: a whole 4x8x8 slice. The times are simulated.
512 devices in a mesh: ctx: 32 (over z, y_hi), heads: 16 (over y_lo, x, core).
Axes of the slice: x: 4, y: 8 (y_hi: 4, y_lo: 2; y = y_hi * 2 + y_lo), z: 8, core: 2. Of those that a mesh axis runs over, the one named last changes fastest.
Arguments:
- resid_in: bfloat16 [4096, 5376], P('ctx', 'heads'), may hold values from -6 to 6
- first_layer_queries: bfloat16 [4096, 4096], P('ctx', 'heads'), may hold values from -270 to 270
- first_layer_keys: bfloat16 [4096, 2048], P('ctx', 'heads'), may hold values from -7 to 7
- first_layer_values: bfloat16 [4096, 2048], P('ctx', 'heads'), may hold values from -6 to 6
- out_one: bfloat16 [4096, 5376], P('heads'), may hold values from -6 to 6
- post_gain: float32 [5376], replicated, may hold values from 0.1 to 1.9
- pre_gain: float32 [5376], replicated, may hold values from 0.1 to 1.9
- proj_query: bfloat16 [5376, 4096], P('ctx', 'heads'), may hold values from -30 to 30
- key_projection: bfloat16 [5376, 2048], P('ctx', 'heads'), may hold values from -1 to 1
- value_projection: bfloat16 [5376, 2048], P('ctx', 'heads'), may hold values from -0.078125 to 0.078125
- window: int32 [32], P('heads'), may hold values from 512 to 1024, as said below
- positions: int32 [4096], replicated, may hold values from 0 to 2047, as said below
Outputs:
- resid_out: bfloat16 [4096, 5376], P('ctx', 'heads')
- attended: bfloat16 [4096, 4096], P('ctx', 'heads')
Inputs may be any that keep to these rules, and one draw needn't show every extreme that they name: Each query head's window counts back from and includes its own token; some head's window is exactly 1024. `positions`: tokens form three packed documents: a position is 0 at a document's first token and one more than the previous token's otherwise; one document has exactly 2048 tokens and none has more.
All inputs are finite; a program needn't handle non-finite values.
Results may differ from a plain program's by a relative error of at most 0.03.
Values may be sent and summed in bfloat16 or wider, within the bound.
No kernel may reach another device: no remote copies, remote signals or barrier semaphores. Data moves between devices by JAX's collectives and lax.ppermute only.
A program may use at most 64 MiB of HBM per device.

v0:
```python
from functools import partial
import jax
import jax.numpy as jnp
from jax import lax
from jax.sharding import PartitionSpec as P

HEAD_SIZE = 128
LONGEST_WINDOW = 1024
SCALE = 168.0 ** (-0.5)
EPS = 1e-06
THETA = 1000000.0
POSITION_FACTOR = 0.125


def shifted(value, axis, steps):
    count = lax.axis_size(axis)
    leading, last = (max(0, -steps), min(count, count - steps))
    return lax.ppermute(value, axis, [(source, source + steps) for source in range(leading, last)])


def from_partner(block, axis, bit):
    count = lax.axis_size(axis)
    route = []
    for low in range(count):
        high = low | 1 << bit
        if high != low and high < count:
            route += [(low, high), (high, low)]
    return lax.ppermute(block, axis, route)


def apply_rotary(values, pos_rows, factor):
    half_dim = values.shape[-1] // 2
    speeds = THETA ** (-(jnp.arange(half_dim, dtype=jnp.float32) * 2.0 / values.shape[-1]))
    angles = (pos_rows.astype(jnp.float32) * factor)[:, None] * speeds[None, :]
    cosine = jnp.cos(angles)[:, None, :]
    sine_part = jnp.sin(angles)[:, None, :]
    front_half = values[..., :half_dim]
    back_half = values[..., half_dim:]
    return jnp.concatenate(
        [front_half * cosine - back_half * sine_part, back_half * cosine + front_half * sine_part],
        axis=-1,
    )


def lookup(position_table, tokens):
    return jnp.take(position_table, jnp.clip(tokens, 0, position_table.shape[0] - 1))


def zig_token(row_ids, tok_dev):
    half_rows = tok_dev // 2
    device_of = row_ids // tok_dev
    local_row = row_ids % tok_dev
    last_pair = 2 * lax.axis_size("ctx") - 1
    return jnp.where(
        local_row < half_rows,
        2 * device_of * half_rows + local_row,
        (last_pair - 2 * device_of) * half_rows + local_row - half_rows,
    )


def masked_attention(
    query_row_block,
    key_row_block,
    value_row_block,
    query_tok,
    key_tok,
    query_pos,
    key_pos,
    window_limits,
):
    scores = (
        jnp.einsum(
            "qagd,kad->qagk", query_row_block, key_row_block, preferred_element_type=jnp.float32
        )
        * SCALE
    )
    distance = query_tok[:, None] - key_tok[None, :]
    base_ok = (
        (distance >= 0)
        & (key_tok[None, :] >= 0)
        & (query_pos[:, None] - key_pos[None, :] == distance)
    )
    visible = base_ok[:, None, None, :] & (
        distance[:, None, None, :] < window_limits[None, :, :, None]
    )
    row_peak = jnp.max(jnp.where(visible, scores, -1e30), axis=-1, keepdims=True)
    lifted = jnp.where(visible, jnp.exp(scores - row_peak), 0.0)
    row_total = jnp.sum(lifted, axis=-1)
    mixed = jnp.einsum(
        "qagk,kad->qagd",
        lifted.astype(jnp.bfloat16),
        value_row_block,
        preferred_element_type=jnp.float32,
    )
    return (mixed / row_total[..., None]).astype(jnp.bfloat16)


def mirror(rows_block, mover):
    half_rows = rows_block.shape[0] // 2
    travel = rows_block[half_rows:]
    bit_count = lax.axis_size("ctx").bit_length() - 1
    for bit_index in range(bit_count):
        travel = mover(travel, bit_index)
    return jnp.concatenate([rows_block[:half_rows], travel], axis=0)


def project(residual_rows, pre_gain, proj_query, key_projection, value_projection, row_pos):
    row_count = residual_rows.shape[0]
    widened = residual_rows.astype(jnp.float32)
    normalized_rows = (
        pre_gain[None, :]
        * widened
        * lax.rsqrt(jnp.mean(widened * widened, axis=1, keepdims=True) + EPS)
    ).astype(jnp.bfloat16)
    query_heads = proj_query.shape[1] // HEAD_SIZE
    pair_heads = key_projection.shape[1] // HEAD_SIZE
    second_layer_query = (
        apply_rotary(
            jnp.dot(
                normalized_rows,
                lax.all_gather(proj_query, "ctx", axis=0, tiled=True),
                preferred_element_type=jnp.float32,
            ).reshape(row_count, query_heads, HEAD_SIZE),
            row_pos,
            POSITION_FACTOR,
        )
        .astype(jnp.bfloat16)
        .reshape(row_count, query_heads * HEAD_SIZE)
    )
    second_layer_key = (
        apply_rotary(
            jnp.dot(
                normalized_rows,
                lax.all_gather(key_projection, "ctx", axis=0, tiled=True),
                preferred_element_type=jnp.float32,
            ).reshape(row_count, pair_heads, HEAD_SIZE),
            row_pos,
            POSITION_FACTOR,
        )
        .astype(jnp.bfloat16)
        .reshape(row_count, pair_heads * HEAD_SIZE)
    )
    second_layer_value = jnp.dot(
        normalized_rows,
        lax.all_gather(value_projection, "ctx", axis=0, tiled=True),
        preferred_element_type=jnp.float32,
    ).astype(jnp.bfloat16)
    return (second_layer_query, second_layer_key, second_layer_value)


def attend_block(
    state, query_row_block, key_block, value_block, query_tok, query_pos, block_tok, block_pos
):
    row_peak, row_total, weighted = state
    scores = (
        jnp.einsum("qagd,kad->qagk", query_row_block, key_block, preferred_element_type=jnp.float32)
        * SCALE
    )
    distance = query_tok[:, None] - block_tok[None, :]
    visible = (distance >= 0) & (query_pos[:, None] - block_pos[None, :] == distance)
    visible = visible[:, None, None, :]
    new_peak = jnp.maximum(row_peak, jnp.max(jnp.where(visible, scores, -1e30), axis=-1))
    lifted = jnp.where(visible, jnp.exp(scores - new_peak[..., None]), 0.0)
    shrink = jnp.exp(row_peak - new_peak)
    row_total = row_total * shrink + jnp.sum(lifted, axis=-1)
    weighted = weighted * shrink[..., None] + jnp.einsum(
        "qagk,kad->qagd",
        lifted.astype(jnp.bfloat16),
        value_block,
        preferred_element_type=jnp.float32,
    )
    return (new_peak, row_total, weighted)


def keep_state(state):
    return state


def shards(
    resid_in,
    first_layer_queries,
    first_layer_keys,
    first_layer_values,
    out_one,
    post_gain,
    pre_gain,
    proj_query,
    key_projection,
    value_projection,
    window,
    positions,
):
    tok_dev = resid_in.shape[0]
    col_width = resid_in.shape[1]
    ctx_place = lax.axis_index("ctx")
    head_place = lax.axis_index("heads")
    query_heads = first_layer_queries.shape[1] // HEAD_SIZE
    pair_heads = first_layer_keys.shape[1] // HEAD_SIZE
    group_length = query_heads // pair_heads
    window_limits = window.reshape(pair_heads, group_length)
    own_pairs = jnp.stack([first_layer_keys, first_layer_values])
    reach_count = LONGEST_WINDOW // tok_dev
    pieces = [own_pairs]
    for section in range(reach_count):
        pieces = [shifted(own_pairs, "ctx", section + 1)] + pieces
    extended = jnp.concatenate(pieces, axis=1)
    key_span = extended.shape[1]
    local_tok = ctx_place * tok_dev + jnp.arange(tok_dev, dtype=jnp.int32)
    key_tok = (ctx_place - reach_count) * tok_dev + jnp.arange(key_span, dtype=jnp.int32)
    attend_one = masked_attention(
        first_layer_queries.reshape(tok_dev, pair_heads, group_length, HEAD_SIZE),
        extended[0].reshape(key_span, pair_heads, HEAD_SIZE),
        extended[1].reshape(key_span, pair_heads, HEAD_SIZE),
        local_tok,
        key_tok,
        lookup(positions, local_tok),
        lookup(positions, key_tok),
        window_limits,
    )
    attend_one = attend_one.reshape(tok_dev, query_heads * HEAD_SIZE)
    partial_rows = jnp.dot(attend_one, out_one, preferred_element_type=jnp.float32)
    mirror_tok = zig_token(ctx_place * tok_dev + jnp.arange(tok_dev, dtype=jnp.int32), tok_dev)
    mirror_pos = lookup(positions, mirror_tok)
    summed = lax.psum(partial_rows.astype(jnp.bfloat16), "heads").astype(jnp.float32)
    post_scaled = summed * lax.rsqrt(jnp.mean(summed * summed, axis=1, keepdims=True) + EPS)
    resid_full = lax.all_gather(resid_in, "heads", axis=1, tiled=True)
    residual_rows = (resid_full.astype(jnp.float32) + post_gain[None, :] * post_scaled).astype(
        jnp.bfloat16
    )
    resid_out = lax.dynamic_slice_in_dim(residual_rows, head_place * col_width, col_width, 1)
    second_layer_query, second_layer_key, second_layer_value = project(
        residual_rows,
        pre_gain,
        proj_query,
        key_projection,
        value_projection,
        lookup(positions, local_tok),
    )
    merged = jnp.concatenate([second_layer_query, second_layer_key, second_layer_value], axis=1)

    def move_proj(piece, bit_index):
        return from_partner(piece, "ctx", bit_index)

    merged = mirror(merged, move_proj)
    query_cols = query_heads * HEAD_SIZE
    pair_cols = pair_heads * HEAD_SIZE
    second_layer_query = merged[:, :query_cols]
    second_layer_key = merged[:, query_cols : query_cols + pair_cols]
    second_layer_value = merged[:, query_cols + pair_cols :]
    half_rows = tok_dev // 2
    queries = second_layer_query.reshape(tok_dev, pair_heads, group_length, HEAD_SIZE)
    query_parts = (queries[:half_rows], queries[half_rows:])
    tok_parts = (mirror_tok[:half_rows], mirror_tok[half_rows:])
    pos_parts = (mirror_pos[:half_rows], mirror_pos[half_rows:])
    pair_two = jnp.stack([second_layer_key, second_layer_value])

    def empty_state():
        return (
            jnp.full((half_rows, pair_heads, group_length), -1e30, jnp.float32),
            jnp.zeros((half_rows, pair_heads, group_length), jnp.float32),
            jnp.zeros((half_rows, pair_heads, group_length, HEAD_SIZE), jnp.float32),
        )

    start_state = (empty_state(), empty_state())
    piece = lax.all_gather(pair_two, "ctx", axis=1, tiled=True)
    piece_rows = piece.shape[1]
    unit_rows = 2 * tok_dev
    unit_count = piece_rows // unit_rows

    def one_unit(index, state):
        offset = index * unit_rows
        unit_block = lax.dynamic_slice_in_dim(piece, offset, unit_rows, 1)
        current = list(state)
        for key_half in range(unit_rows // half_rows):
            key_block = unit_block[0, key_half * half_rows : (key_half + 1) * half_rows].reshape(
                half_rows, pair_heads, HEAD_SIZE
            )
            value_block = unit_block[1, key_half * half_rows : (key_half + 1) * half_rows].reshape(
                half_rows, pair_heads, HEAD_SIZE
            )
            key_row_block = offset + key_half * half_rows + jnp.arange(half_rows, dtype=jnp.int32)
            block_tok = zig_token(key_row_block, tok_dev)
            block_pos = lookup(positions, block_tok)
            earliest = jnp.min(block_tok)
            for query_half in range(2):
                work = partial(
                    attend_block,
                    query_row_block=query_parts[query_half],
                    key_block=key_block,
                    value_block=value_block,
                    query_tok=tok_parts[query_half],
                    query_pos=pos_parts[query_half],
                    block_tok=block_tok,
                    block_pos=block_pos,
                )
                needed = earliest <= tok_parts[query_half][half_rows - 1]
                current[query_half] = lax.cond(needed, work, keep_state, current[query_half])
        return tuple(current)

    final_state = lax.fori_loop(0, unit_count, one_unit, start_state)
    front = final_state[0][2] / final_state[0][1][..., None]
    back = final_state[1][2] / final_state[1][1][..., None]
    attended = (
        jnp.concatenate([front, back], axis=0)
        .astype(jnp.bfloat16)
        .reshape(tok_dev, query_heads * HEAD_SIZE)
    )
    return (resid_out, attended)


def solution(mesh):
    placed = (
        P("ctx", "heads"),
        P("ctx", "heads"),
        P("ctx", "heads"),
        P("ctx", "heads"),
        P("heads", None),
        P(),
        P(),
        P("ctx", "heads"),
        P("ctx", "heads"),
        P("ctx", "heads"),
        P("heads"),
        P(),
    )
    return jax.shard_map(
        shards,
        mesh=mesh,
        in_specs=placed,
        out_specs=(P("ctx", "heads"), P("ctx", "heads")),
        check_vma=False,
    )
```

profile of v0, /device:TPU:2, one launch (start us, length us, event | category | flops | bytes accessed | tf_op | source)
XLA Modules:
  0.0 968.1 jit_solution(9957120319989894820)
XLA Ops:
  8.2 6.1 collective-permute-start
  14.3 8.0 collective-permute-start.1
  22.2 7.7 collective-permute-start.2
  30.0 5.4 collective-permute-start.3
  35.4 3.4 collective-permute-start.4
  40.6 6.5 gather_fusion.4
  48.5 2.3 collective-permute-start.5
  50.8 6.6 collective-permute-start.6
  59.3 1.8 collective-permute-done.7
  62.5 1.8 convolution_convert_fusion
  67.2 123.5 %all-reduce.2.cloned.1.call-done = bf16[128,5376]{1,0:T(8,128)(2,1)} async-done(((bf16[128,5376]{1,0:T(8,128)(2,1)}), bf16[128,5376]{1,0:T(8,128)(2,1)}) %all-reduce.2.cloned.1.call-update) | async-done | bytes 1376272 | tf_op jit(solution)/shard_map/psum | solution.py:224
  192.4 41.8 %all-gather.6.cloned.1.call-done = bf16[128,5376]{0,1:T(8,128)(2,1)} async-done(((bf16[128,336]{0,1:T(8,128)(2,1)}), bf16[128,5376]{0,1:T(8,128)(2,1)}) %all-gather.6.cloned.1.call-update) | async-done | bytes 1376272 | tf_op jit(solution)/shard_map/all_gather | solution.py:226
  234.3 2.5 copy.63
  236.8 3.8 fusion.130
  240.6 81.4 %all-gather.10.cloned.1.call-done = bf16[5376,128]{1,0:T(8,128)(2,1)} async-done(((bf16[168,128]{1,0:T(8,128)(2,1)}), bf16[5376,128]{1,0:T(8,128)(2,1)}) %all-gather.10.cloned.1.call-update) | async-done | bytes 1376272 | tf_op jit(solution)/shard_map/all_gather | solution.py:134
  322.0 2.5 convolution_bitcast_fusion.9
  324.7 80.3 %all-gather.12.cloned.1.call-done = bf16[5376,128]{1,0:T(8,128)(2,1)} async-done(((bf16[168,128]{1,0:T(8,128)(2,1)}), bf16[5376,128]{1,0:T(8,128)(2,1)}) %all-gather.12.cloned.1.call-update) | async-done | bytes 1376272 | tf_op jit(solution)/shard_map/all_gather | solution.py:145
  405.0 2.5 convolution_convert_fusion.1
  407.6 86.1 %all-gather.8.cloned.1.call-done = bf16[5376,256]{1,0:T(8,128)(2,1)} async-done(((bf16[168,256]{1,0:T(8,128)(2,1)}), bf16[5376,256]{1,0:T(8,128)(2,1)}) %all-gather.8.cloned.1.call-update) | async-done | bytes 2752528 | tf_op jit(solution)/shard_map/all_gather | solution.py:121
  493.7 3.4 fusion.164
  497.3 4.5 collective-permute-start.8
  501.9 4.6 collective-permute-done.8
  506.5 4.3 collective-permute-start.9
  510.8 7.9 collective-permute-done.9
  518.7 2.6 collective-permute-start.10
  521.3 5.4 collective-permute-done.10
  526.6 1.9 collective-permute-start.11
  528.6 10.0 %collective-permute-done.11 = bf16[64,512]{0,1:T(8,128)(2,1)S(1)} collective-permute-done((bf16[64,512]{0,1:T(8,128)(2,1)S(1)}, bf16[64,512]{0,1:T(8,128)(2,1)S(1)}, u32[]{:S(2)}, u32[]{:S(2)}) %collective-permute-start.11) | collective-permute-done | bytes 65568 | tf_op jit(solution)/shard_map/ppermute | solution.py:28
  538.6 4.0 collective-permute-start.12
  542.6 7.1 collective-permute-done.12
  553.8 75.9 %all-gather.14.cloned.1.call-done = bf16[2,4096,128]{1,2,0:T(8,128)(2,1)} async-done(((bf16[2,128,128]{1,2,0:T(8,128)(2,1)}), bf16[2,4096,128]{1,2,0:T(8,128)(2,1)}) %all-gather.14.cloned.1.call-update) | async-done | bytes 2097168 | tf_op jit(solution)/shard_map/all_gather | solution.py:265
  629.8 330.5 %while.26 = (s32[]{:T(128)}, f32[64,1,2]{0,2,1:T(2,128)S(1)}, f32[64,1,2]{0,2,1:T(2,128)S(1)}, f32[64,1,2,128]{3,0,2,1:T(8,128)S(1)}, f32[64,1,2]{0,2,1:T(2,128)...) while((s32[]{:T(128)}, f32[64,1,2]{0,2,1:T(2,128)S(1)}, ...), condition=%wide.region_42.45_spmd, body=%wide.region_5.44_spmd.sunk | while | flops 34610448 | bytes 3114491 | solution.py:300
  (1144 shorter events, 213.9 us)
Async XLA Ops:
  7.2 55.4 %copy-start = (bf16[256,5376]{1,0:T(8,128)(2,1)S(1)}, bf16[256,5376]{1,0:T(8,128)(2,1)}, u32[]{:S(2)}) copy-start(bf16[256,5376]{1,0:T(8,128)(2,1)} %param.38) | copy-start | bytes 8257540
  7.2 33.4 %copy-start.1 = (s32[4096]{0:T(1024)S(1)}, s32[4096]{0:T(1024)}, u32[]{:S(2)}) copy-start(s32[4096]{0:T(1024)} %param.45) | copy-start | bytes 49156
  7.2 183.5 %all-reduce.2.cloned.1.call-start = ((), (), s32[]{:S(2)}) async-start(), calls=%async_computation.1 | async-start | bytes 2752512 | tf_op jit(solution)/shard_map/psum | solution.py:224
  8.2 40.3 %collective-permute-start = (bf16[2,128,128]{2,1,0:T(8,128)(2,1)S(1)}, bf16[2,128,128]{2,1,0:T(8,128)(2,1)S(1)}, u32[]{:S(2)}, u32[]{:S(2)}) collective-permute-start(bf16[2,128,128]{2,1,0:T(8,128)(2,1)S(1)} %pad_maximum_fusion.2), channel_id=1, source_target_pairs={{0,128},{16,144},{32,160},{48,176},{64,192},{80,208},{96,224},{112... | collective-permute-start | bytes 196616 | tf_op jit(solution)/shard_map/ppermute | solution.py:18
  14.3 36.5 %collective-permute-start.1 = (bf16[2,128,128]{2,1,0:T(8,128)(2,1)S(1)}, bf16[2,128,128]{2,1,0:T(8,128)(2,1)S(1)}, u32[]{:S(2)}, u32[]{:S(2)}) collective-permute-start(bf16[2,128,128]{2,1,0:T(8,128)(2,1)S(1)} %pad_maximum_fusion.2), channel_id=1, source_target_pairs={{0,112},{16,128},{32,144},{48,160},{64,176},{80,192},{96,208},{112... | collective-permute-start | bytes 196616 | tf_op jit(solution)/shard_map/ppermute | solution.py:18
  22.2 35.1 %collective-permute-start.2 = (bf16[2,128,128]{2,1,0:T(8,128)(2,1)S(1)}, bf16[2,128,128]{2,1,0:T(8,128)(2,1)S(1)}, u32[]{:S(2)}, u32[]{:S(2)}) collective-permute-start(bf16[2,128,128]{2,1,0:T(8,128)(2,1)S(1)} %pad_maximum_fusion.2), channel_id=1, source_target_pairs={{0,96},{16,112},{32,128},{48,144},{64,160},{80,176},{96,192},{112,... | collective-permute-start | bytes 196616 | tf_op jit(solution)/shard_map/ppermute | solution.py:18
  30.0 28.7 %collective-permute-start.3 = (bf16[2,128,128]{2,1,0:T(8,128)(2,1)S(1)}, bf16[2,128,128]{2,1,0:T(8,128)(2,1)S(1)}, u32[]{:S(2)}, u32[]{:S(2)}) collective-permute-start(bf16[2,128,128]{2,1,0:T(8,128)(2,1)S(1)} %pad_maximum_fusion.2), channel_id=1, source_target_pairs={{0,80},{16,96},{32,112},{48,128},{64,144},{80,160},{96,176},{112,1... | collective-permute-start | bytes 196616 | tf_op jit(solution)/shard_map/ppermute | solution.py:18
  35.4 23.3 %collective-permute-start.4 = (bf16[2,128,128]{2,1,0:T(8,128)(2,1)S(1)}, bf16[2,128,128]{2,1,0:T(8,128)(2,1)S(1)}, u32[]{:S(2)}, u32[]{:S(2)}) collective-permute-start(bf16[2,128,128]{2,1,0:T(8,128)(2,1)S(1)} %pad_maximum_fusion.2), channel_id=1, source_target_pairs={{0,64},{16,80},{32,96},{48,112},{64,128},{80,144},{96,160},{112,17... | collective-permute-start | bytes 196616 | tf_op jit(solution)/shard_map/ppermute | solution.py:18
  47.1 14.0 %copy-start.2 = (bf16[128,128]{1,0:T(8,128)(2,1)S(1)}, bf16[128,128]{1,0:T(8,128)(2,1)}, u32[]{:S(2)}) copy-start(bf16[128,128]{1,0:T(8,128)(2,1)} %param.37) | copy-start | bytes 98308
  47.1 14.0 %copy-start.3 = (bf16[128,128]{1,0:T(8,128)(2,1)S(1)}, bf16[128,128]{1,0:T(8,128)(2,1)}, u32[]{:S(2)}) copy-start(bf16[128,128]{1,0:T(8,128)(2,1)} %param.36) | copy-start | bytes 98308
  47.1 14.0 %copy-start.5 = (s32[2]{0:T(128)S(1)}, s32[2]{0:T(128)}, u32[]{:S(2)}) copy-start(s32[2]{0:T(128)} %param.44) | copy-start | bytes 28
  47.1 14.0 %copy-start.6 = (bf16[128,256]{1,0:T(8,128)(2,1)S(1)}, bf16[128,256]{1,0:T(8,128)(2,1)}, u32[]{:S(2)}) copy-start(bf16[128,256]{1,0:T(8,128)(2,1)} %param.35) | copy-start | bytes 196612
  48.5 10.3 %collective-permute-start.5 = (bf16[2,128,128]{2,1,0:T(8,128)(2,1)S(1)}, bf16[2,128,128]{2,1,0:T(8,128)(2,1)S(1)}, u32[]{:S(2)}, u32[]{:S(2)}) collective-permute-start(bf16[2,128,128]{2,1,0:T(8,128)(2,1)S(1)} %pad_maximum_fusion.2), channel_id=1, source_target_pairs={{0,48},{16,64},{32,80},{48,96},{64,112},{80,128},{96,144},{112,160... | collective-permute-start | bytes 196616 | tf_op jit(solution)/shard_map/ppermute | solution.py:18
  50.8 8.5 collective-permute-start.6
  57.4 3.7 collective-permute-start.7
  64.3 169.9 %all-gather.6.cloned.1.call-start = ((), (), s32[]{:S(2)}) async-start(), calls=%async_computation | async-start | bytes 1462272 | tf_op jit(solution)/shard_map/all_gather | solution.py:226
  65.1 256.9 %all-gather.10.cloned.1.call-start = ((), (), s32[]{:S(2)}) async-start(), calls=%async_computation.3 | async-start | bytes 1419264 | tf_op jit(solution)/shard_map/all_gather | solution.py:134
  65.8 339.2 %all-gather.12.cloned.1.call-start = ((), (), s32[]{:S(2)}) async-start(), calls=%async_computation.4 | async-start | bytes 1419264 | tf_op jit(solution)/shard_map/all_gather | solution.py:145
  66.4 427.3 %all-gather.8.cloned.1.call-start = ((), (), s32[]{:S(2)}) async-start(), calls=%async_computation.2 | async-start | bytes 2838528 | tf_op jit(solution)/shard_map/all_gather | solution.py:121
  67.0 562.7 %all-gather.14.cloned.1.call-start = ((), (), s32[]{:S(2)}) async-start(), calls=%async_computation.5 | async-start | bytes 2162688 | tf_op jit(solution)/shard_map/all_gather | solution.py:265
  192.4 44.4 %copy-start.4 = (f32[5376]{0:T(1024)S(1)}, f32[5376]{0:T(1024)}, u32[]{:S(2)}) copy-start(f32[5376]{0:T(1024)} %param.39) | copy-start | bytes 64516
  236.8 85.2 %copy-start.7 = (f32[5376]{0:T(1024)S(1)}, f32[5376]{0:T(1024)}, u32[]{:S(2)}) copy-start(f32[5376]{0:T(1024)} %param.40) | copy-start | bytes 64516
  497.3 9.2 collective-permute-start.8
  506.5 12.2 %collective-permute-start.9 = (bf16[64,512]{0,1:T(8,128)(2,1)S(1)}, bf16[64,512]{0,1:T(8,128)(2,1)S(1)}, u32[]{:S(2)}, u32[]{:S(2)}) collective-permute-start(bf16[64,512]{0,1:T(8,128)(2,1)S(1)} %collective-permute-done.8), channel_id=1, source_target_pairs={{0,32},{32,0},{16,48},{48,16},{64,96},{96,64},{80,112},{112,80},{1... | collective-permute-start | bytes 196616 | tf_op jit(solution)/shard_map/ppermute | solution.py:28
  518.7 8.0 collective-permute-start.10
  526.6 12.0 %collective-permute-start.11 = (bf16[64,512]{0,1:T(8,128)(2,1)S(1)}, bf16[64,512]{0,1:T(8,128)(2,1)S(1)}, u32[]{:S(2)}, u32[]{:S(2)}) collective-permute-start(bf16[64,512]{0,1:T(8,128)(2,1)S(1)} %collective-permute-done.10), channel_id=1, source_target_pairs={{0,128},{128,0},{16,144},{144,16},{32,160},{160,32},{48,176},{176,... | collective-permute-start | bytes 196616 | tf_op jit(solution)/shard_map/ppermute | solution.py:28
  538.6 11.1 %collective-permute-start.12 = (bf16[64,512]{0,1:T(8,128)(2,1)S(1)}, bf16[64,512]{0,1:T(8,128)(2,1)S(1)}, u32[]{:S(2)}, u32[]{:S(2)}) collective-permute-start(bf16[64,512]{0,1:T(8,128)(2,1)S(1)} %collective-permute-done.11), channel_id=1, source_target_pairs={{0,256},{256,0},{16,272},{272,16},{32,288},{288,32},{48,304},{304,... | collective-permute-start | bytes 196616 | tf_op jit(solution)/shard_map/ppermute | solution.py:28
Sparse Core Ops, SparseCore 0:
  64.5 126.2 all-reduce.1
  192.9 41.3 all-gather.5
  237.5 84.5 all-gather.9
  325.1 79.9 all-gather.11
  408.1 85.5 all-gather.7
  550.6 79.0 all-gather.13
where the time goes:
time: 972 us; the launch traced here: 968 us
  waiting for transfers between devices  529 us (54%)
  loops' own time  173 us (18%)
  local copies, waits for them, and re-layouts  113 us (12%)
  starting transfers between devices  58.4 us (6%)
  other arithmetic  44 us (5%)
  matrix products  36.2 us (4%)
  between operations  14.7 us (2%)
    another operation x1, loops' own time, shards(): final_state = lax.fori_loop(0, unit_count, one_unit, start_state)  169 us
    psum x1, waiting for transfers between devices, shards(): lax.psum(partial_rows.astype(jnp.bfloat16), 'heads').astype(jnp.float32)  123 us
    all_gather x1, waiting for transfers between devices, project(): lax.all_gather(proj_query, 'ctx', axis=0, tiled=True)  86.1 us
    all_gather x1, waiting for transfers between devices, project(): lax.all_gather(key_projection, 'ctx', axis=0, tiled=True)  81.4 us
    all_gather x1, waiting for transfers between devices, project(): lax.all_gather(value_projection, 'ctx', axis=0, tiled=True)  80.3 us
    all_gather x1, waiting for transfers between devices, shards(): piece = lax.all_gather(pair_two, 'ctx', axis=1, tiled=True)  75.9 us
    gather x67, local copies, waits for them, and re-layouts, lookup(): jnp.take(position_table, jnp.clip(tokens, 0, position_table.shape[0] - 1))  58.9 us
    all_gather x1, waiting for transfers between devices, shards(): resid_full = lax.all_gather(resid_in, 'heads', axis=1, tiled=True)  41.8 us
  transfers between devices with their start and end apart: 19, of which 13 were waited for; matrix products, arithmetic and copies ran while one was open for 3% of the time, Pallas kernels for 0%

commit v1 on v0

--- a/solution.py
+++ b/solution.py
@@ -10,6 +10,12 @@
 EPS = 1e-06
 THETA = 1000000.0
 POSITION_FACTOR = 0.125
+
+
+def add_all(x, name):
+    parts = lax.all_gather(x, name, axis=0, tiled=False)
+    total = parts.sum(axis=0)
+    return total
 
 
 def shifted(value, axis, steps):
@@ -221,7 +227,7 @@
     partial_rows = jnp.dot(attend_one, out_one, preferred_element_type=jnp.float32)
     mirror_tok = zig_token(ctx_place * tok_dev + jnp.arange(tok_dev, dtype=jnp.int32), tok_dev)
     mirror_pos = lookup(positions, mirror_tok)
-    summed = lax.psum(partial_rows.astype(jnp.bfloat16), "heads").astype(jnp.float32)
+    summed = add_all(partial_rows.astype(jnp.bfloat16), "heads").astype(jnp.float32)
     post_scaled = summed * lax.rsqrt(jnp.mean(summed * summed, axis=1, keepdims=True) + EPS)
     resid_full = lax.all_gather(resid_in, "heads", axis=1, tiled=True)
     residual_rows = (resid_full.astype(jnp.float32) + post_gain[None, :] * post_scaled).astype(

time: 972 us -> 926 us (0.953)
  waiting for transfers between devices: 529 us -> 479 us
  other arithmetic: 44 us -> 58.2 us
    psum x1 -> x0, waiting for transfers between devices: 123 us -> none  [shards(): lax.psum(partial_rows.astype(jnp.bfloat16), 'heads').astype(jnp.float32)]
    all_gather x0 -> x1, waiting for transfers between devices: none -> 121 us  [add_all(): parts = lax.all_gather(x, name, axis=0, tiled=False)]
    all_gather x1, waiting for transfers between devices: 41.8 us -> 3.76 us  [shards(): resid_full = lax.all_gather(resid_in, 'heads', axis=1, tiled=True)]
    reduce_sum x0 -> x1, other arithmetic: none -> 13.3 us  [add_all(): total = parts.sum(axis=0)]
    all_gather x1, waiting for transfers between devices: 86.1 us -> 75.6 us  [project(): lax.all_gather(proj_query, 'ctx', axis=0, tiled=True)]
  transfers between devices with their start and end apart: 19 -> 19, of which waited for: 13 -> 13; matrix products, arithmetic and copies ran while one was open for 3% -> 5% of each run, Pallas kernels for 0% -> 0%
where the time goes in v1:
time: 926 us; the launch traced here: 922 us
  waiting for transfers between devices  479 us (52%)
  loops' own time  164 us (18%)
  local copies, waits for them, and re-layouts  111 us (12%)
  starting transfers between devices  58.4 us (6%)
  other arithmetic  58.2 us (6%)
  matrix products  36.3 us (4%)
  between operations  14.7 us (2%)
    another operation x1, loops' own time, shards(): final_state = lax.fori_loop(0, unit_count, one_unit, start_state)  160 us
    all_gather x1, waiting for transfers between devices, add_all(): parts = lax.all_gather(x, name, axis=0, tiled=False)  121 us
    all_gather x1, waiting for transfers between devices, project(): lax.all_gather(key_projection, 'ctx', axis=0, tiled=True)  80.6 us
    all_gather x1, waiting for transfers between devices, project(): lax.all_gather(value_projection, 'ctx', axis=0, tiled=True)  80.3 us
    all_gather x1, waiting for transfers between devices, shards(): piece = lax.all_gather(pair_two, 'ctx', axis=1, tiled=True)  79.6 us
    all_gather x1, waiting for transfers between devices, project(): lax.all_gather(proj_query, 'ctx', axis=0, tiled=True)  75.6 us
    gather x67, local copies, waits for them, and re-layouts, lookup(): jnp.take(position_table, jnp.clip(tokens, 0, position_table.shape[0] - 1))  58.9 us
    ppermute x8, starting transfers between devices, shifted(): lax.ppermute(value, axis, [(source, source + steps) for source in range(l...  40.7 us
  transfers between devices with their start and end apart: 19, of which 13 were waited for; matrix products, arithmetic and copies ran while one was open for 5% of the time, Pallas kernels for 0%

profile of v1, /device:TPU:2, one launch (start us, length us, event | category | flops | bytes accessed | tf_op | source)
XLA Modules:
  0.0 921.9 jit_solution(10366004065899394700)
XLA Ops:
  8.2 6.1 collective-permute-start
  14.3 8.0 collective-permute-start.1
  22.2 7.7 collective-permute-start.2
  30.0 5.4 collective-permute-start.3
  35.4 3.4 collective-permute-start.4
  40.6 6.5 gather_fusion.4
  48.5 2.3 collective-permute-start.5
  50.8 6.6 collective-permute-start.6
  66.6 3.8 all-gather.8.cloned.1.call-done
  70.3 2.5 copy.80
  72.9 121.4 %all-gather.18.cloned.1.call-done = bf16[2048,5376]{1,0:T(8,128)(2,1)} async-done(((bf16[128,5376]{1,0:T(8,128)(2,1)}), bf16[2048,5376]{1,0:T(8,128)(2,1)}) %all-gather.18.cloned.1.call-update) | async-done | bytes 22020112 | tf_op jit(solution)/shard_map/all_gather | solution.py:16
  194.3 13.3 %reduce_sum.128 = bf16[128,5376]{1,0:T(8,128)(2,1)} reduce(bf16[16,128,5376]{2,1,0:T(8,128)(2,1)} %bitcast.407, bf16[]{:T(256)} %constant.435.clone.1), dimensions={0}, to_apply=%region_2.4 | reduce | flops 10321920 | bytes 23396354 | tf_op jit(solution)/shard_map/reduce_sum | solution.py:17
  207.6 1.8 fusion.124
  209.4 3.3 fusion.130
  212.7 75.6 %all-gather.10.cloned.1.call-done = bf16[5376,256]{1,0:T(8,128)(2,1)} async-done(((bf16[168,256]{1,0:T(8,128)(2,1)}), bf16[5376,256]{1,0:T(8,128)(2,1)}) %all-gather.10.cloned.1.call-update) | async-done | bytes 2752528 | tf_op jit(solution)/shard_map/all_gather | solution.py:127
  288.4 3.4 fusion.164
  291.8 80.6 %all-gather.12.cloned.1.call-done = bf16[5376,128]{1,0:T(8,128)(2,1)} async-done(((bf16[168,128]{1,0:T(8,128)(2,1)}), bf16[5376,128]{1,0:T(8,128)(2,1)}) %all-gather.12.cloned.1.call-update) | async-done | bytes 1376272 | tf_op jit(solution)/shard_map/all_gather | solution.py:140
  372.5 2.5 convolution_bitcast_fusion.9
  375.2 80.3 %all-gather.14.cloned.1.call-done = bf16[5376,128]{1,0:T(8,128)(2,1)} async-done(((bf16[168,128]{1,0:T(8,128)(2,1)}), bf16[5376,128]{1,0:T(8,128)(2,1)}) %all-gather.14.cloned.1.call-update) | async-done | bytes 1376272 | tf_op jit(solution)/shard_map/all_gather | solution.py:151
  455.5 2.5 convolution_convert_fusion.1
  458.1 4.4 collective-permute-start.8
  462.5 4.8 collective-permute-done.8
  467.3 4.7 collective-permute-start.9
  472.0 7.3 collective-permute-done.9
  479.3 2.7 collective-permute-start.10
  481.9 5.4 collective-permute-done.10
  487.3 1.9 collective-permute-start.11
  489.2 9.0 collective-permute-done.11
  498.3 3.9 collective-permute-start.12
  502.2 7.3 collective-permute-done.12
  513.6 79.6 %all-gather.16.cloned.1.call-done = bf16[2,4096,128]{1,2,0:T(8,128)(2,1)} async-done(((bf16[2,128,128]{1,2,0:T(8,128)(2,1)}), bf16[2,4096,128]{1,2,0:T(8,128)(2,1)}) %all-gather.16.cloned.1.call-update) | async-done | bytes 2097168 | tf_op jit(solution)/shard_map/all_gather | solution.py:271
  593.3 320.9 %while.26 = (s32[]{:T(128)}, f32[64,1,2]{0,2,1:T(2,128)S(1)}, f32[64,1,2]{0,2,1:T(2,128)S(1)}, f32[64,1,2,128]{3,0,2,1:T(8,128)S(1)}, f32[64,1,2]{0,2,1:T(2,128)...) while((s32[]{:T(128)}, f32[64,1,2]{0,2,1:T(2,128)S(1)}, ...), condition=%wide.region_42.45_spmd, body=%wide.region_5.44_spmd.sunk | while | flops 34610448 | bytes 3114491 | solution.py:306
  (1147 shorter events, 213.9 us)
Async XLA Ops:
  7.2 55.5 %copy-start = (bf16[256,5376]{1,0:T(8,128)(2,1)S(1)}, bf16[256,5376]{1,0:T(8,128)(2,1)}, u32[]{:S(2)}) copy-start(bf16[256,5376]{1,0:T(8,128)(2,1)} %param.38) | copy-start | bytes 8257540
  7.2 33.5 %copy-start.1 = (s32[4096]{0:T(1024)S(1)}, s32[4096]{0:T(1024)}, u32[]{:S(2)}) copy-start(s32[4096]{0:T(1024)} %param.45) | copy-start | bytes 49156
  7.2 63.1 %all-gather.8.cloned.1.call-start = ((), (), s32[]{:S(2)}) async-start(), calls=%async_computation | async-start | bytes 1462272 | tf_op jit(solution)/shard_map/all_gather | solution.py:232
  8.2 40.4 %collective-permute-start = (bf16[2,128,128]{2,1,0:T(8,128)(2,1)S(1)}, bf16[2,128,128]{2,1,0:T(8,128)(2,1)S(1)}, u32[]{:S(2)}, u32[]{:S(2)}) collective-permute-start(bf16[2,128,128]{2,1,0:T(8,128)(2,1)S(1)} %pad_maximum_fusion.2), channel_id=1, source_target_pairs={{0,128},{16,144},{32,160},{48,176},{64,192},{80,208},{96,224},{112... | collective-permute-start | bytes 196616 | tf_op jit(solution)/shard_map/ppermute | solution.py:24
  14.3 36.6 %collective-permute-start.1 = (bf16[2,128,128]{2,1,0:T(8,128)(2,1)S(1)}, bf16[2,128,128]{2,1,0:T(8,128)(2,1)S(1)}, u32[]{:S(2)}, u32[]{:S(2)}) collective-permute-start(bf16[2,128,128]{2,1,0:T(8,128)(2,1)S(1)} %pad_maximum_fusion.2), channel_id=1, source_target_pairs={{0,112},{16,128},{32,144},{48,160},{64,176},{80,192},{96,208},{112... | collective-permute-start | bytes 196616 | tf_op jit(solution)/shard_map/ppermute | solution.py:24
  22.2 35.2 %collective-permute-start.2 = (bf16[2,128,128]{2,1,0:T(8,128)(2,1)S(1)}, bf16[2,128,128]{2,1,0:T(8,128)(2,1)S(1)}, u32[]{:S(2)}, u32[]{:S(2)}) collective-permute-start(bf16[2,128,128]{2,1,0:T(8,128)(2,1)S(1)} %pad_maximum_fusion.2), channel_id=1, source_target_pairs={{0,96},{16,112},{32,128},{48,144},{64,160},{80,176},{96,192},{112,... | collective-permute-start | bytes 196616 | tf_op jit(solution)/shard_map/ppermute | solution.py:24
  30.0 28.8 %collective-permute-start.3 = (bf16[2,128,128]{2,1,0:T(8,128)(2,1)S(1)}, bf16[2,128,128]{2,1,0:T(8,128)(2,1)S(1)}, u32[]{:S(2)}, u32[]{:S(2)}) collective-permute-start(bf16[2,128,128]{2,1,0:T(8,128)(2,1)S(1)} %pad_maximum_fusion.2), channel_id=1, source_target_pairs={{0,80},{16,96},{32,112},{48,128},{64,144},{80,160},{96,176},{112,1... | collective-permute-start | bytes 196616 | tf_op jit(solution)/shard_map/ppermute | solution.py:24
  35.4 23.4 %collective-permute-start.4 = (bf16[2,128,128]{2,1,0:T(8,128)(2,1)S(1)}, bf16[2,128,128]{2,1,0:T(8,128)(2,1)S(1)}, u32[]{:S(2)}, u32[]{:S(2)}) collective-permute-start(bf16[2,128,128]{2,1,0:T(8,128)(2,1)S(1)} %pad_maximum_fusion.2), channel_id=1, source_target_pairs={{0,64},{16,80},{32,96},{48,112},{64,128},{80,144},{96,160},{112,17... | collective-permute-start | bytes 196616 | tf_op jit(solution)/shard_map/ppermute | solution.py:24
  38.8 155.5 %all-gather.18.cloned.1.call-start = ((), (), s32[]{:S(2)}) async-start(), calls=%async_computation.5 | async-start | bytes 23396352 | tf_op jit(solution)/shard_map/all_gather | solution.py:16
  47.1 14.0 %copy-start.3 = (bf16[128,128]{1,0:T(8,128)(2,1)S(1)}, bf16[128,128]{1,0:T(8,128)(2,1)}, u32[]{:S(2)}) copy-start(bf16[128,128]{1,0:T(8,128)(2,1)} %param.37) | copy-start | bytes 98308
  47.1 14.0 %copy-start.4 = (bf16[128,128]{1,0:T(8,128)(2,1)S(1)}, bf16[128,128]{1,0:T(8,128)(2,1)}, u32[]{:S(2)}) copy-start(bf16[128,128]{1,0:T(8,128)(2,1)} %param.36) | copy-start | bytes 98308
  47.2 14.0 %copy-start.6 = (s32[2]{0:T(128)S(1)}, s32[2]{0:T(128)}, u32[]{:S(2)}) copy-start(s32[2]{0:T(128)} %param.44) | copy-start | bytes 28
  47.2 14.0 %copy-start.7 = (bf16[128,256]{1,0:T(8,128)(2,1)S(1)}, bf16[128,256]{1,0:T(8,128)(2,1)}, u32[]{:S(2)}) copy-start(bf16[128,256]{1,0:T(8,128)(2,1)} %param.35) | copy-start | bytes 196612
  48.5 10.3 %collective-permute-start.5 = (bf16[2,128,128]{2,1,0:T(8,128)(2,1)S(1)}, bf16[2,128,128]{2,1,0:T(8,128)(2,1)S(1)}, u32[]{:S(2)}, u32[]{:S(2)}) collective-permute-start(bf16[2,128,128]{2,1,0:T(8,128)(2,1)S(1)} %pad_maximum_fusion.2), channel_id=1, source_target_pairs={{0,48},{16,64},{32,80},{48,96},{64,112},{80,128},{96,144},{112,160... | collective-permute-start | bytes 196616 | tf_op jit(solution)/shard_map/ppermute | solution.py:24
  50.8 8.5 collective-permute-start.6
  57.4 3.7 collective-permute-start.7
  64.4 224.0 %all-gather.10.cloned.1.call-start = ((), (), s32[]{:S(2)}) async-start(), calls=%async_computation.1 | async-start | bytes 2838528 | tf_op jit(solution)/shard_map/all_gather | solution.py:127
  65.1 307.3 %all-gather.12.cloned.1.call-start = ((), (), s32[]{:S(2)}) async-start(), calls=%async_computation.2 | async-start | bytes 1419264 | tf_op jit(solution)/shard_map/all_gather | solution.py:140
  65.7 389.8 %all-gather.14.cloned.1.call-start = ((), (), s32[]{:S(2)}) async-start(), calls=%async_computation.3 | async-start | bytes 1419264 | tf_op jit(solution)/shard_map/all_gather | solution.py:151
  66.3 526.9 %all-gather.16.cloned.1.call-start = ((), (), s32[]{:S(2)}) async-start(), calls=%async_computation.4 | async-start | bytes 2162688 | tf_op jit(solution)/shard_map/all_gather | solution.py:271
  194.3 15.1 %copy-start.5 = (f32[5376]{0:T(1024)S(1)}, f32[5376]{0:T(1024)}, u32[]{:S(2)}) copy-start(f32[5376]{0:T(1024)} %param.39) | copy-start | bytes 64516
  207.6 1.8 copy-start.2
  209.4 78.9 %copy-start.8 = (f32[5376]{0:T(1024)S(1)}, f32[5376]{0:T(1024)}, u32[]{:S(2)}) copy-start(f32[5376]{0:T(1024)} %param.40) | copy-start | bytes 64516
  458.1 9.2 collective-permute-start.8
  467.3 12.0 %collective-permute-start.9 = (bf16[64,512]{0,1:T(8,128)(2,1)S(1)}, bf16[64,512]{0,1:T(8,128)(2,1)S(1)}, u32[]{:S(2)}, u32[]{:S(2)}) collective-permute-start(bf16[64,512]{0,1:T(8,128)(2,1)S(1)} %collective-permute-done.8), channel_id=1, source_target_pairs={{0,32},{32,0},{16,48},{48,16},{64,96},{96,64},{80,112},{112,80},{1... | collective-permute-start | bytes 196616 | tf_op jit(solution)/shard_map/ppermute | solution.py:34
  479.3 8.1 collective-permute-start.10
  487.3 11.0 %collective-permute-start.11 = (bf16[64,512]{0,1:T(8,128)(2,1)S(1)}, bf16[64,512]{0,1:T(8,128)(2,1)S(1)}, u32[]{:S(2)}, u32[]{:S(2)}) collective-permute-start(bf16[64,512]{0,1:T(8,128)(2,1)S(1)} %collective-permute-done.10), channel_id=1, source_target_pairs={{0,128},{128,0},{16,144},{144,16},{32,160},{160,32},{48,176},{176,... | collective-permute-start | bytes 196616 | tf_op jit(solution)/shard_map/ppermute | solution.py:34
  498.3 11.2 %collective-permute-start.12 = (bf16[64,512]{0,1:T(8,128)(2,1)S(1)}, bf16[64,512]{0,1:T(8,128)(2,1)S(1)}, u32[]{:S(2)}, u32[]{:S(2)}) collective-permute-start(bf16[64,512]{0,1:T(8,128)(2,1)S(1)} %collective-permute-done.11), channel_id=1, source_target_pairs={{0,256},{256,0},{16,272},{272,16},{32,288},{288,32},{48,304},{304,... | collective-permute-start | bytes 196616 | tf_op jit(solution)/shard_map/ppermute | solution.py:34
Sparse Core Ops, SparseCore 0:
  38.9 31.3 all-gather.7
  72.5 121.8 all-gather.17
  197.5 90.8 all-gather.9
  291.4 81.0 all-gather.11
  375.5 79.9 all-gather.13
  510.4 82.7 all-gather.15
